TPU v7x, 32 devices: a whole 2x2x4 slice. The times are simulated.
32 devices in a mesh: layer: 4 (over y, core), feat: 8 (over z, x).
Axes of the slice: x: 2, y: 2, z: 4, core: 2. Of those that a mesh axis runs over, the one named last changes fastest.
Arguments:
- acts: bfloat16 [4, 768, 1024], P('layer'), may hold values from -6 to 6
- targets: bfloat16 [4, 768, 1024], P('layer', 'feat'), may hold values from -6 to 6
- enc_weight: bfloat16 [4, 1024, 20480], P('layer', None, 'feat'), may hold values from -0.1875 to 0.1875
- enc_bias: float32 [4, 20480], P('layer', 'feat'), may hold values from -3 to 3
- dec_weight: bfloat16 [4, 20480, 2, 1024], P('layer', 'feat'), may hold values from -0.0390625 to 0.0390625
- dec_bias: float32 [4, 1024], P('layer'), may hold values from -3 to 3
Outputs:
- errors: float32 [4, 768, 1024], P('layer', 'feat')
- enc_grad: bfloat16 [4, 1024, 20480], P('layer', None, 'feat')
All inputs are finite; a program needn't handle non-finite values.
Results may differ from a plain program's by a relative error of at most 0.006.
Values may be sent and summed in bfloat16 or wider, within the bound.
A program may use at most 128 MiB of HBM per device.

v0:
```python
import jax
import jax.numpy as jnp
from jax import lax
from jax.sharding import PartitionSpec as P


def passed_along(block, axis, distance):
    devices = range(lax.axis_size(axis))
    route = [(i - distance, i) for i in devices if i - distance in devices]
    return lax.ppermute(block, axis, route)


def contract_width(errs, decoder):
    return lax.dot_general(
        errs, decoder, (((1,), (1,)), ((), ())), preferred_element_type=jnp.float32
    )


def local(acts, targets, enc_weight, enc_bias, dec_weight, dec_bias):
    inputs = acts[0]
    wanted = targets[0]
    weight = enc_weight[0]
    bias = enc_bias[0]
    decoder = dec_weight[0]
    out_bias = dec_bias[0]
    tokens = inputs.shape[0]
    pre = jnp.dot(inputs, weight, preferred_element_type=jnp.float32) + bias
    latent = (jax.nn.softplus(4.0 * pre) * 0.25).astype(jnp.bfloat16)
    first_dec = decoder[:, 0, :]
    second_dec = decoder[:, 1, :]
    later = jnp.dot(latent, second_dec, preferred_element_type=jnp.float32)
    arrived = passed_along(later, "layer", 1)
    own = jnp.dot(latent, first_dec, preferred_element_type=jnp.float32)
    recon = lax.psum_scatter(own + arrived, "feat", scatter_dimension=0, tiled=True)
    errors = recon + out_bias - wanted.astype(jnp.float32)
    err_half = errors.astype(jnp.bfloat16)
    deriv = jax.nn.sigmoid(4.0 * pre)
    scale = tokens ** (-0.5)
    gathered = lax.all_gather(err_half, "feat", axis=0, tiled=True)
    following = passed_along(gathered, "layer", -1)
    grad_latent = contract_width(gathered, first_dec) + contract_width(following, second_dec)
    grad_pre = (grad_latent * deriv).astype(jnp.bfloat16)
    total = lax.dot_general(
        inputs, grad_pre, (((0,), (0,)), ((), ())), preferred_element_type=jnp.float32
    )
    enc_grad = (total * scale).astype(jnp.bfloat16)
    return (errors[None], enc_grad[None])


def solution(mesh):
    return jax.shard_map(
        local,
        mesh=mesh,
        in_specs=(
            P("layer", None, None),
            P("layer", "feat", None),
            P("layer", None, "feat"),
            P("layer", "feat"),
            P("layer", "feat", None, None),
            P("layer", None),
        ),
        out_specs=(P("layer", "feat", None), P("layer", None, "feat")),
        check_vma=False,
    )
```

profile of v0, /device:TPU:1, one launch (start us, length us, event | category | flops | bytes accessed | tf_op | source)
XLA Modules:
  0.0 256.6 jit_solution(2426340068791333634)
XLA Ops:
  7.2 0.0 copy-start
  7.2 0.0 copy-start.3
  7.2 0.0 reduce-scatter.2.cloned.1.call-start
  7.2 11.4 %copy.12 = bf16[1,2560,2,1024]{3,1,2,0:T(8,128)(2,1)} copy(bf16[1,2560,2,1024]{3,2,1,0:T(2,128)(2,1)} %param.10) | data formatting | bytes 20971520 | tf_op args[4]
  18.6 0.0 copy-done.3
  18.7 0.0 copy-done
  18.7 0.0 copy-start.1
  18.7 6.3 %fusion.2 = f32[768,2560]{1,0:T(8,128)S(1)} fusion(bf16[1,1024,2560]{2,1,0:T(8,128)(2,1)} %param.8, bf16[1,768,1024]{2,1,0:T(8,128)(2,1)S(1)} %copy-done), kind=kOutput, calls=%fused_computation.9 | convolution fusion | flops 4026531840 | bytes 14680064 | tf_op jit(solution)/shard_map/dot_general | solution.py:27
  25.0 0.0 copy-start.5
  25.0 0.0 copy-done.1
  25.0 7.8 %fusion.7 = f32[768,1024]{1,0:T(8,128)S(1)} fusion(bf16[2560,2,1024]{2,0,1:T(8,128)(2,1)S(1)} %bitcast.38, f32[768,2560]{1,0:T(8,128)S(1)} %fusion.2, f32[2560]{0:T(1024)S(1)} %reduce), kind=kOutput, calls=%fused_computation.14 | convolution fusion | flops 4046192640 | bytes 16265216 | tf_op jit(solution)/shard_map/dot_general | solution.py:31
  32.9 0.0 copy-start.2
  32.9 0.0 copy-start.4
  32.9 4.8 %collective-permute-start = (f32[768,1024]{1,0:T(8,128)S(1)}, f32[768,1024]{1,0:T(8,128)S(1)}, u32[]{:S(2)}, u32[]{:S(2)}) collective-permute-start(f32[768,1024]{1,0:T(8,128)S(1)} %fusion.7), channel_id=1, source_target_pairs={{0,8},{8,16},{16,24},{1,9},{9,17},{17,25},{2,10},{10,18},{18,26},{... | collective-permute-start | bytes 9437192 | tf_op jit(solution)/shard_map/ppermute | solution.py:10
  37.7 34.0 %collective-permute-done = f32[768,1024]{1,0:T(8,128)S(1)} collective-permute-done((f32[768,1024]{1,0:T(8,128)S(1)}, f32[768,1024]{1,0:T(8,128)S(1)}, u32[]{:S(2)}, u32[]{:S(2)}) %collective-permute-start) | collective-permute-done | bytes 3145760 | tf_op jit(solution)/shard_map/ppermute | solution.py:10
  71.8 0.0 copy-done.5
  71.8 9.6 %fusion.8 = f32[768,1024]{1,0:T(8,128)} fusion(f32[768,1024]{1,0:T(8,128)S(1)} %collective-permute-done, bf16[2560,2,1024]{2,0,1:T(8,128)(2,1)S(1)} %bitcast.39, f32[768,2560]{1,0:T(8,128)S(1)} %fusion.2, f32[2560]{0:T(1024)S(1)} %reduce), kind=kOutput, calls=%fused_computation.15 | convolution fusion | flops 4046979072 | bytes 19410944 | tf_op jit(solution)/shard_map/dot_general | solution.py:33
  81.4 0.0 reduce-scatter.2.cloned.1.call-update
  81.4 0.0 all-gather.2.cloned.1.call-start
  81.4 75.7 %reduce-scatter.2.cloned.1.call-done = f32[96,1024]{1,0:T(8,128)} async-done(((f32[768,1024]{1,0:T(8,128)}), f32[96,1024]{1,0:T(8,128)}) %reduce-scatter.2.cloned.1.call-update) | async-done | bytes 393232 | tf_op jit(solution)/shard_map/reduce_scatter | solution.py:34
  157.1 0.0 copy-done.2
  157.1 0.0 copy-done.4
  157.1 1.9 fusion.11
  159.0 0.0 all-gather.2.cloned.1.call-update
  159.0 43.8 %all-gather.2.cloned.1.call-done = bf16[768,1024]{1,0:T(8,128)(2,1)} async-done(((bf16[96,1024]{1,0:T(8,128)(2,1)}), bf16[768,1024]{1,0:T(8,128)(2,1)}) %all-gather.2.cloned.1.call-update) | async-done | bytes 1572880 | tf_op jit(solution)/shard_map/all_gather | solution.py:39
  202.9 3.8 %collective-permute-start.1 = (bf16[768,1024]{1,0:T(8,128)(2,1)}, bf16[768,1024]{1,0:T(8,128)(2,1)S(1)}, u32[]{:S(2)}, u32[]{:S(2)}) collective-permute-start(bf16[768,1024]{1,0:T(8,128)(2,1)} %all-gather.2.cloned.1.call-done), channel_id=1, source_target_pairs={{8,0},{16,8},{24,16},{9,1},{17,9},{25,17},{10,2},{18,10},{26,18},{... | collective-permute-start | bytes 4718600 | tf_op jit(solution)/shard_map/ppermute | solution.py:10
  206.7 10.4 %fusion.5 = f32[768,2560]{1,0:T(8,128)} fusion(bf16[768,1024]{1,0:T(8,128)(2,1)} %all-gather.2.cloned.1.call-done, bf16[2560,2,1024]{2,0,1:T(8,128)(2,1)} %bitcast.36), kind=kOutput, calls=%fused_computation.12 | convolution fusion | flops 4026531840 | bytes 14680064 | tf_op jit(solution)/shard_map/dot_general | solution.py:14
  217.1 8.8 %collective-permute-done.1 = bf16[768,1024]{1,0:T(8,128)(2,1)S(1)} collective-permute-done((bf16[768,1024]{1,0:T(8,128)(2,1)}, bf16[768,1024]{1,0:T(8,128)(2,1)S(1)}, u32[]{:S(2)}, u32[]{:S(2)}) %collective-permute-start.1) | collective-permute-done | bytes 1572896 | tf_op jit(solution)/shard_map/ppermute | solution.py:10
  225.8 16.0 %fusion.4 = bf16[1,1024,2560]{1,2,0:T(8,128)(2,1)} fusion(f32[768,2560]{1,0:T(8,128)} %fusion.5, f32[768,2560]{1,0:T(8,128)} %copy-done.5, bf16[768,1024]{1,0:T(8,128)(2,1)S(1)} %collective-permute-done.1, bf16[2560,2,1024]{2,0,1:T(8,128)(2,1)} %bitcast.37, f32[2560]{0:T(1024)S(1)} %reduce, bf16[1,768,1024]{2,1,0:T(8,128)(2,1)S(1)} %copy-done), kind=kOutput, calls=%fused_computation.11 | convolution fusion | flops 8074035200 | bytes 29370368 | tf_op jit(solution)/shard_map/dot_general | solution.py:43
  241.9 7.9 %copy.10 = bf16[1,1024,2560]{2,1,0:T(8,128)(2,1)} copy(bf16[1,1024,2560]{1,2,0:T(8,128)(2,1)} %fusion.4) | data formatting | bytes 10485760
  (1 shorter events, 0.0 us)
Async XLA Ops:
  7.2 11.5 %copy-start = (bf16[1,768,1024]{2,1,0:T(8,128)(2,1)S(1)}, bf16[1,768,1024]{2,1,0:T(8,128)(2,1)}, u32[]{:S(2)}) copy-start(bf16[1,768,1024]{2,1,0:T(8,128)(2,1)} %param.6) | copy-start | bytes 4718596
  7.2 11.5 %copy-start.3 = (f32[1,2560]{1,0:T(1,128)S(1)}, f32[1,2560]{1,0:T(1,128)}, u32[]{:S(2)}) copy-start(f32[1,2560]{1,0:T(1,128)} %param.9) | copy-start | bytes 30724
  7.2 149.9 %reduce-scatter.2.cloned.1.call-start = ((), (), s32[]{:S(2)}) async-start(), calls=%async_computation.1 | async-start | bytes 3538944 | tf_op jit(solution)/shard_map/reduce_scatter | solution.py:34
  18.7 6.3 %copy-start.1 = (bf16[1,2560,2,1024]{3,1,2,0:T(8,128)(2,1)S(1)}, bf16[1,2560,2,1024]{3,1,2,0:T(8,128)(2,1)}, u32[]{:S(2)}) copy-start(bf16[1,2560,2,1024]{3,1,2,0:T(8,128)(2,1)} %copy.12) | copy-start | bytes 31457284
  25.0 46.7 %copy-start.5 = (f32[768,2560]{1,0:T(8,128)}, f32[768,2560]{1,0:T(8,128)S(1)}, u32[]{:S(2)}) copy-start(f32[768,2560]{1,0:T(8,128)S(1)} %fusion.2) | copy-start | bytes 23592964
  32.9 124.3 %copy-start.2 = (bf16[1,96,1024]{2,1,0:T(8,128)(2,1)S(1)}, bf16[1,96,1024]{2,1,0:T(8,128)(2,1)}, u32[]{:S(2)}) copy-start(bf16[1,96,1024]{2,1,0:T(8,128)(2,1)} %param.7) | copy-start | bytes 589828
  32.9 124.2 %copy-start.4 = (f32[1,1024]{1,0:T(1,128)S(1)}, f32[1,1024]{1,0:T(1,128)}, u32[]{:S(2)}) copy-start(f32[1,1024]{1,0:T(1,128)} %param.11) | copy-start | bytes 12292
  32.9 38.9 %collective-permute-start = (f32[768,1024]{1,0:T(8,128)S(1)}, f32[768,1024]{1,0:T(8,128)S(1)}, u32[]{:S(2)}, u32[]{:S(2)}) collective-permute-start(f32[768,1024]{1,0:T(8,128)S(1)} %fusion.7), channel_id=1, source_target_pairs={{0,8},{8,16},{16,24},{1,9},{9,17},{17,25},{2,10},{10,18},{18,26},{... | collective-permute-start | bytes 9437192 | tf_op jit(solution)/shard_map/ppermute | solution.py:10
  81.4 121.5 %all-gather.2.cloned.1.call-start = ((), (), s32[]{:S(2)}) async-start(), calls=%async_computation.2 | async-start | bytes 1769472 | tf_op jit(solution)/shard_map/all_gather | solution.py:39
  202.9 23.0 %collective-permute-start.1 = (bf16[768,1024]{1,0:T(8,128)(2,1)}, bf16[768,1024]{1,0:T(8,128)(2,1)S(1)}, u32[]{:S(2)}, u32[]{:S(2)}) collective-permute-start(bf16[768,1024]{1,0:T(8,128)(2,1)} %all-gather.2.cloned.1.call-done), channel_id=1, source_target_pairs={{8,0},{16,8},{24,16},{9,1},{17,9},{25,17},{10,2},{18,10},{26,18},{... | collective-permute-start | bytes 4718600 | tf_op jit(solution)/shard_map/ppermute | solution.py:10
Sparse Core Ops, SparseCore 0:
  81.5 75.5 reduce-scatter.1
  159.9 42.9 all-gather.1
where the time goes:
time: 257 us
  waiting for transfers between devices  162 us (63%)
  matrix products  50.2 us (20%)
  local copies, waits for them, and re-layouts  19.4 us (8%)
  between operations  14.1 us (5%)
  starting transfers between devices  8.73 us (3%)
    reduce_scatter x1, waiting for transfers between devices, local(): lax.psum_scatter(own + arrived, 'feat', scatter_dimension=0, tiled=True)  75.7 us
    all_gather x1, waiting for transfers between devices, local(): gathered = lax.all_gather(err_half, 'feat', axis=0, tiled=True)  43.8 us
    ppermute x2, waiting for transfers between devices, passed_along(): return lax.ppermute(block, axis, route)  42.8 us
    unnamed x14, local copies, waits for them, and re-layouts  19.4 us
    dot_general x1, matrix products, local(): lax.dot_general(inputs, grad_pre, (((0,), (0,)), ((), ())), preferred_ele...  16 us
    dot_general x1, matrix products, contract_width(): lax.dot_general(errs, decoder, (((1,), (1,)), ((), ())), preferred_elemen...  10.4 us
    dot_general x1, matrix products, local(): own = jnp.dot(latent, first_dec, preferred_element_type=jnp.float32)  9.61 us
    ppermute x2, starting transfers between devices, passed_along(): return lax.ppermute(block, axis, route)  8.65 us
  transfers between devices with their start and end apart: 4, of which 4 were waited for; matrix products, arithmetic and copies ran while one was open for 4% of the time, Pallas kernels for 0%

commit v1 on v0

v1 whole, which is shorter than its diff:
```python
import functools

import jax
import jax.numpy as jnp
from jax import lax
from jax.experimental import pallas as pl
from jax.experimental.pallas import tpu as pltpu
from jax.sharding import PartitionSpec as P

MESH = pl.DeviceIdType.MESH
CHUNKS = 4


def exchange_kernel(
    layers, n, latent_ref, dec_ref, targets_ref, bias_ref,
    errors_ref, gath_ref, foll_ref,
    dec, later, arrived, sums, parts,
    dec_sem, up_send, up_recv, rs_send, rs_recv, ag_send, ag_recv, down_send, down_recv,
):
    layer = lax.axis_index("layer")
    me = lax.axis_index("feat")
    above = lax.rem(layer + 1, layers)
    below = lax.rem(layer + layers - 1, layers)
    tokens, width = gath_ref.shape
    rows = tokens // n
    wide = width // CHUNKS

    def peer(k):
        return lax.rem(me + k, n)

    def rows_of(i):
        return pl.ds(pl.multiple_of(i * rows, rows), rows)

    def cols(c):
        return pl.ds(pl.multiple_of(c * wide, wide), wide)

    def load(w, c):
        return pltpu.make_async_copy(
            dec_ref.at[w, :, cols(c)], dec.at[w, :, cols(c)], dec_sem.at[w, c]
        )

    def remote(src, dst, send, recv, where):
        return pltpu.make_async_remote_copy(
            src_ref=src, dst_ref=dst, send_sem=send, recv_sem=recv,
            device_id=where, device_id_type=MESH,
        )

    def up(c):
        return remote(later.at[:, cols(c)], arrived.at[:, cols(c)], up_send.at[c], up_recv.at[c], (above, me))

    def scatter(c, k):
        to = peer(k)
        return remote(
            sums.at[rows_of(to), cols(c)], parts.at[k - 1, :, cols(c)],
            rs_send.at[c, k - 1], rs_recv.at[c, k - 1], (layer, to),
        )

    def gather(c, k, owner):
        spot = gath_ref.at[rows_of(owner), cols(c)]
        return remote(spot, spot, ag_send.at[c, k - 1], ag_recv.at[c, k - 1], (layer, peer(k)))

    def down(c, k, owner):
        return remote(
            gath_ref.at[rows_of(owner), cols(c)], foll_ref.at[rows_of(owner), cols(c)],
            down_send.at[c, k], down_recv.at[c, k], (below, me),
        )

    for w in (1, 0):
        for c in range(CHUNKS):
            load(w, c).start()

    barrier = pltpu.get_barrier_semaphore()
    for k in range(1, n):
        pl.semaphore_signal(barrier, inc=1, device_id=(layer, peer(k)), device_id_type=MESH)
    pl.semaphore_signal(barrier, inc=1, device_id=(above, me), device_id_type=MESH)
    pl.semaphore_signal(barrier, inc=1, device_id=(below, me), device_id_type=MESH)
    pl.semaphore_wait(barrier, n + 1)

    @pl.loop(0, CHUNKS)
    def _(c):
        load(1, c).wait()
        later[:, cols(c)] = jnp.dot(
            latent_ref[...], dec[1, :, cols(c)], preferred_element_type=jnp.float32
        ).astype(jnp.bfloat16)
        up(c).start()

    @pl.loop(0, CHUNKS)
    def _(c):
        load(0, c).wait()
        own = jnp.dot(latent_ref[...], dec[0, :, cols(c)], preferred_element_type=jnp.float32)
        up(c).wait_recv()
        carried = jnp.where(layer > 0, arrived[:, cols(c)].astype(jnp.float32), 0.0)
        sums[:, cols(c)] = (own + carried).astype(jnp.bfloat16)
        for k in range(1, n):
            scatter(c, k).start()

    @pl.loop(0, CHUNKS)
    def _(c):
        total = sums[rows_of(me), cols(c)].astype(jnp.float32)
        for k in range(1, n):
            scatter(c, k).wait_recv()
            total = total + parts[k - 1, :, cols(c)].astype(jnp.float32)
        errors = total + bias_ref[:, cols(c)] - targets_ref[:, cols(c)].astype(jnp.float32)
        errors_ref[:, cols(c)] = errors
        gath_ref[rows_of(me), cols(c)] = errors.astype(jnp.bfloat16)
        for k in range(1, n):
            gather(c, k, me).start()
        down(c, 0, me).start()

    @pl.loop(0, CHUNKS)
    def _(c):
        for k in range(1, n):
            owner = lax.rem(me + n - k, n)
            gather(c, k, owner).wait_recv()
            down(c, k, owner).start()

    @pl.loop(0, CHUNKS)
    def _(c):
        up(c).wait_send()
        for k in range(1, n):
            scatter(c, k).wait_send()
            gather(c, k, me).wait_send()
        for k in range(n):
            owner = lax.rem(me + n - k, n)
            down(c, k, owner).wait_recv()
            down(c, k, owner).wait_send()

    @pl.when(layer == layers - 1)
    def _():
        foll_ref[...] = jnp.zeros_like(foll_ref)


def exchange(layers, n, latent, dec, targets, bias):
    tokens, features = latent.shape
    width = dec.shape[2]
    rows = tokens // n
    half = jnp.bfloat16
    vmem = pl.BlockSpec(memory_space=pltpu.VMEM)
    dma = pltpu.SemaphoreType.DMA
    return pl.pallas_call(
        functools.partial(exchange_kernel, layers, n),
        out_shape=(
            jax.ShapeDtypeStruct((rows, width), jnp.float32),
            jax.ShapeDtypeStruct((tokens, width), half),
            jax.ShapeDtypeStruct((tokens, width), half),
        ),
        in_specs=[vmem, pl.BlockSpec(memory_space=pl.ANY), vmem, vmem],
        out_specs=(vmem, vmem, vmem),
        scratch_shapes=[
            pltpu.VMEM((2, features, width), half),
            pltpu.VMEM((tokens, width), half),
            pltpu.VMEM((tokens, width), half),
            pltpu.VMEM((tokens, width), half),
            pltpu.VMEM((n - 1, rows, width), half),
            dma((2, CHUNKS)),
            dma((CHUNKS,)),
            dma((CHUNKS,)),
            dma((CHUNKS, n - 1)),
            dma((CHUNKS, n - 1)),
            dma((CHUNKS, n - 1)),
            dma((CHUNKS, n - 1)),
            dma((CHUNKS, n)),
            dma((CHUNKS, n)),
        ],
        compiler_params=pltpu.CompilerParams(
            collective_id=0, has_side_effects=True, vmem_limit_bytes=48 * 2**20
        ),
        name="exchange",
    )(latent, dec, targets, bias)


def contract_width(errs, decoder):
    return lax.dot_general(
        errs, decoder, (((1,), (1,)), ((), ())), preferred_element_type=jnp.float32
    )


def local(layers, n, acts, targets, enc_weight, enc_bias, dec_weight, dec_bias):
    inputs = acts[0]
    weight = enc_weight[0]
    bias = enc_bias[0]
    dec = jnp.transpose(dec_weight[0], (1, 0, 2))
    tokens = inputs.shape[0]
    pre = jnp.dot(inputs, weight, preferred_element_type=jnp.float32) + bias
    latent = (jax.nn.softplus(4.0 * pre) * 0.25).astype(jnp.bfloat16)
    errors, gathered, following = exchange(layers, n, latent, dec, targets[0], dec_bias)
    deriv = jax.nn.sigmoid(4.0 * pre)
    scale = tokens ** (-0.5)
    grad_latent = contract_width(gathered, dec[0]) + contract_width(following, dec[1])
    grad_pre = (grad_latent * deriv).astype(jnp.bfloat16)
    total = lax.dot_general(
        inputs, grad_pre, (((0,), (0,)), ((), ())), preferred_element_type=jnp.float32
    )
    enc_grad = (total * scale).astype(jnp.bfloat16)
    return (errors[None], enc_grad[None])


def solution(mesh):
    return jax.shard_map(
        functools.partial(local, mesh.shape["layer"], mesh.shape["feat"]),
        mesh=mesh,
        in_specs=(
            P("layer", None, None),
            P("layer", "feat", None),
            P("layer", None, "feat"),
            P("layer", "feat"),
            P("layer", "feat", None, None),
            P("layer", None),
        ),
        out_specs=(P("layer", "feat", None), P("layer", None, "feat")),
        check_vma=False,
    )
```

time: 257 us -> 145 us (0.56)
  waiting for transfers between devices: 162 us -> 0 us
  Pallas kernels: 0 us -> 87.6 us
  matrix products: 50.2 us -> 35.5 us
  between operations: 14.1 us -> 0.71 us
  starting transfers between devices: 8.73 us -> 0 us
    pallas_call x0 -> x1, Pallas kernels: none -> 87.6 us  [exchange(): pl.pallas_call(functools.partial(exchange_kernel, layers, n), out_shape=(...]
    reduce_scatter x1 -> x0, waiting for transfers between devices: 75.7 us -> none  [local(): lax.psum_scatter(own + arrived, 'feat', scatter_dimension=0, tiled=True)]
    all_gather x1 -> x0, waiting for transfers between devices: 43.8 us -> none  [local(): gathered = lax.all_gather(err_half, 'feat', axis=0, tiled=True)]
    ppermute x2 -> x0, waiting for transfers between devices: 42.8 us -> none  [passed_along(): return lax.ppermute(block, axis, route)]
    dot_general x2 -> x0, matrix products: 17.4 us -> none  [the longest x1 9.61 us: local(): own = jnp.dot(latent, first_dec, preferred_element_type=jnp.float32)]
    ppermute x2 -> x0, starting transfers between devices: 8.65 us -> none  [passed_along(): return lax.ppermute(block, axis, route)]
    dot_general x1, matrix products: 6.32 us -> 13.1 us  [local(): pre = jnp.dot(inputs, weight, preferred_element_type=jnp.float32) + bias]
    dot_general x1, matrix products: 10.4 us -> 6.47 us  [contract_width(): lax.dot_general(errs, decoder, (((1,), (1,)), ((), ())), preferred_elemen...]
  transfers between devices with their start and end apart: 4 -> 0, of which waited for: 4 -> 0; matrix products, arithmetic and copies ran while one was open for 4% -> 0% of each run, Pallas kernels for 0% -> 0%
where the time goes in v1:
time: 145 us
  Pallas kernels  87.6 us (60%)
  matrix products  35.5 us (24%)
  local copies, waits for them, and re-layouts  20 us (14%)
    pallas_call x1, Pallas kernels, exchange(): pl.pallas_call(functools.partial(exchange_kernel, layers, n), out_shape=(...  87.6 us
    unnamed x15, local copies, waits for them, and re-layouts  20 us
    dot_general x1, matrix products, local(): lax.dot_general(inputs, grad_pre, (((0,), (0,)), ((), ())), preferred_ele...  15.9 us
    dot_general x1, matrix products, local(): pre = jnp.dot(inputs, weight, preferred_element_type=jnp.float32) + bias  13.1 us
    dot_general x1, matrix products, contract_width(): lax.dot_general(errs, decoder, (((1,), (1,)), ((), ())), preferred_elemen...  6.47 us

profile of v1, /device:TPU:1, one launch (start us, length us, event | category | flops | bytes accessed | tf_op | source)
XLA Modules:
  0.0 144.7 jit_solution(11259237955000028104)
XLA Ops:
  0.6 0.0 copy-start
  0.6 0.9 reduce
  1.5 11.3 %copy.11 = bf16[1,2560,2,1024]{3,1,2,0:T(8,128)(2,1)} copy(bf16[1,2560,2,1024]{3,2,1,0:T(2,128)(2,1)} %param.10) | data formatting | bytes 20971520 | tf_op args[4]
  12.8 0.0 slice-start
  12.8 0.0 copy-done
  12.8 0.0 copy-start.1
  12.8 0.0 copy-start.2
  12.8 0.0 slice-start.1
  12.8 0.0 slice-start.2
  12.8 13.1 %fusion.1 = (bf16[768,2560]{1,0:T(8,128)(2,1)}, f32[768,2560]{1,0:T(8,128)}) fusion(f32[2560]{0:T(1024)S(1)} %reduce, bf16[1,1024,2560]{2,1,0:T(8,128)(2,1)} %param.8, bf16[1,768,1024]{2,1,0:T(8,128)(2,1)S(1)} %copy-done), kind=kOutput, calls=%fused_computation.4 | convolution fusion | flops 4046192640 | bytes 18622464 | tf_op jit(solution)/shard_map/dot_general | solution.py:184
  26.0 0.0 copy-done.1
  26.0 0.0 copy-done.2
  26.0 87.6 %exchange.1 = (f32[96,1024]{1,0:T(8,128)S(1)}, bf16[768,1024]{1,0:T(8,128)(2,1)S(1)}, bf16[768,1024]{1,0:T(8,128)(2,1)S(1)}) custom-call(bf16[768,2560]{1,0:T(8,128)(2,1)} %get-tuple-element.10.latent_ref, bf16[2,2560,1024]{2,1,0:T(8,128)(2,1)} %bitcast.35, bf16[96,1024]{1,0:T(8,128)(2,1)S(1)} %bitcast.34, f32[1,1024]{1,0:T(1,128)S(1)} %copy-done.2), custom_call_target="tpu_custom_call" | custom-call | tf_op jit(solution)/shard_map/exchange/pallas_call | solution.py:140
  113.6 0.0 slice-done
  113.6 0.0 slice-done.1
  113.6 0.0 slice-done.2
  113.6 6.5 %fusion.2 = f32[768,2560]{1,0:T(8,128)} fusion(bf16[768,1024]{1,0:T(8,128)(2,1)S(1)} %get-tuple-element.6, bf16[2,2560,1024]{2,1,0:T(8,128)(2,1)S(1)} %bitcast.39), kind=kOutput, calls=%fused_computation.9 | convolution fusion | flops 4026531840 | bytes 14680064 | tf_op jit(solution)/shard_map/dot_general | solution.py:173
  120.1 15.9 %fusion.5 = bf16[1,1024,2560]{1,2,0:T(8,128)(2,1)} fusion(f32[768,2560]{1,0:T(8,128)} %fusion.2, f32[768,2560]{1,0:T(8,128)} %get-tuple-element.11, bf16[768,1024]{1,0:T(8,128)(2,1)S(1)} %get-tuple-element.7, bf16[2,2560,1024]{2,1,0:T(8,128)(2,1)} %bitcast.36, f32[2560]{0:T(1024)S(1)} %reduce, bf16[1,768,1024]{2,1,0:T(8,128)(2,1)S(1)} %copy-done), kind=kOutput, calls=%fused_computation.12 | convolution fusion | flops 8074035200 | bytes 29370368 | tf_op jit(solution)/shard_map/dot_general | solution.py:191
  136.0 7.9 %copy.9 = bf16[1,1024,2560]{2,1,0:T(8,128)(2,1)} copy(bf16[1,1024,2560]{1,2,0:T(8,128)(2,1)} %fusion.5) | data formatting | bytes 10485760
  143.9 0.7 copy.13
  (1 shorter events, 0.0 us)
Async XLA Ops:
  0.6 12.2 %copy-start = (bf16[1,768,1024]{2,1,0:T(8,128)(2,1)S(1)}, bf16[1,768,1024]{2,1,0:T(8,128)(2,1)}, u32[]{:S(2)}) copy-start(bf16[1,768,1024]{2,1,0:T(8,128)(2,1)} %param.6) | copy-start | bytes 4718596
  12.8 100.8 %slice-start = ((s8[10485760]{0:T(1024)(128)(4,1)}), s8[4194304]{0:T(1024)(128)(4,1)S(1)}, s32[]{:S(2)}) async-start(s8[10485760]{0:T(1024)(128)(4,1)} %bitcast.37), calls=%async_computation | async-start | bytes 8388608
  12.8 13.2 %copy-start.1 = (bf16[1,96,1024]{2,1,0:T(8,128)(2,1)S(1)}, bf16[1,96,1024]{2,1,0:T(8,128)(2,1)}, u32[]{:S(2)}) copy-start(bf16[1,96,1024]{2,1,0:T(8,128)(2,1)} %param.7) | copy-start | bytes 589828
  12.8 13.2 %copy-start.2 = (f32[1,1024]{1,0:T(1,128)S(1)}, f32[1,1024]{1,0:T(1,128)}, u32[]{:S(2)}) copy-start(f32[1,1024]{1,0:T(1,128)} %bias_ref.1) | copy-start | bytes 12292
  12.8 100.8 %slice-start.1 = ((s8[10485760]{0:T(1024)(128)(4,1)}), s8[4194304]{0:T(1024)(128)(4,1)S(1)}, s32[]{:S(2)}) async-start(s8[10485760]{0:T(1024)(128)(4,1)} %bitcast.37), calls=%async_computation.1 | async-start | bytes 8388608
  12.8 100.8 %slice-start.2 = ((s8[10485760]{0:T(1024)(128)(4,1)}), s8[2097152]{0:T(1024)(128)(4,1)S(1)}, s32[]{:S(2)}) async-start(s8[10485760]{0:T(1024)(128)(4,1)} %bitcast.37), calls=%async_computation.2 | async-start | bytes 4194304

commit v2 on v1

v2 whole, which is shorter than its diff:
```python
import functools

import jax
import jax.numpy as jnp
from jax import lax
from jax.experimental import pallas as pl
from jax.experimental.pallas import tpu as pltpu
from jax.sharding import PartitionSpec as P

MESH = pl.DeviceIdType.MESH
CHUNKS = 4


def inner_of(n):
    return max(d for d in range(1, n + 1) if n % d == 0 and d * d <= n)


def exchange_kernel(
    layers, m, o, latent_ref, dec_ref, targets_ref, bias_ref, acts_ref,
    errors_ref, gath_ref, foll_ref, turned_ref,
    dec, later, arrived, sums, near, mids, far, mine,
    dec_sem, up_send, up_recv, near_send, near_recv, far_send, far_recv,
    out_send, out_recv, in_send, in_recv, down_send, down_recv,
):
    layer = lax.axis_index("layer")
    me = lax.axis_index("feat")
    z, x = me // m, lax.rem(me, m)
    above = lax.rem(layer + 1, layers)
    below = lax.rem(layer + layers - 1, layers)
    tokens, width = gath_ref.shape
    rows = tokens // (m * o)
    wide = width // CHUNKS

    def at(dz, dx):
        return lax.rem(z + dz + o, o) * m + lax.rem(x + dx + m, m)

    def rows_of(i):
        return pl.ds(pl.multiple_of(i * rows, rows), rows)

    def cols(c):
        return pl.ds(pl.multiple_of(c * wide, wide), wide)

    def load(w, c):
        return pltpu.make_async_copy(
            dec_ref.at[w, :, cols(c)], dec.at[w, :, cols(c)], dec_sem.at[w, c]
        )

    def remote(src, dst, send, recv, where):
        return pltpu.make_async_remote_copy(
            src_ref=src, dst_ref=dst, send_sem=send, recv_sem=recv,
            device_id=where, device_id_type=MESH,
        )

    def up(c):
        return remote(later.at[:, cols(c)], arrived.at[:, cols(c)], up_send.at[c], up_recv.at[c], (above, me))

    def add_near(c, q, r):
        j = (q - 1) * o + r
        return remote(
            sums.at[rows_of(at(r, q)), cols(c)], near.at[j, :, cols(c)],
            near_send.at[c, j], near_recv.at[c, j], (layer, at(0, q)),
        )

    def add_far(c, r):
        return remote(
            mids.at[r - 1, :, cols(c)], far.at[r - 1, :, cols(c)],
            far_send.at[c, r - 1], far_recv.at[c, r - 1], (layer, at(r, 0)),
        )

    def give_far(c, r, owner):
        spot = gath_ref.at[rows_of(owner), cols(c)]
        return remote(spot, spot, out_send.at[c, r - 1], out_recv.at[c, r - 1], (layer, at(r, 0)))

    def give_near(c, q, r, owner):
        j = (q - 1) * o + r
        spot = gath_ref.at[rows_of(owner), cols(c)]
        return remote(spot, spot, in_send.at[c, j], in_recv.at[c, j], (layer, at(0, q)))

    def down(c, q, r):
        owner = at(-r, -q)
        j = q * o + r
        return remote(
            gath_ref.at[rows_of(owner), cols(c)], foll_ref.at[rows_of(owner), cols(c)],
            down_send.at[c, j], down_recv.at[c, j], (below, me),
        )

    for w in (1, 0):
        for c in range(CHUNKS):
            load(w, c).start()

    barrier = pltpu.get_barrier_semaphore()
    for to in (
        [(layer, at(0, q)) for q in range(1, m)]
        + [(layer, at(r, 0)) for r in range(1, o)]
        + [(above, me), (below, me)]
    ):
        pl.semaphore_signal(barrier, inc=1, device_id=to, device_id_type=MESH)
    pl.semaphore_wait(barrier, m + o)

    @pl.loop(0, CHUNKS)
    def _(c):
        load(1, c).wait()
        later[:, cols(c)] = jnp.dot(
            latent_ref[...], dec[1, :, cols(c)], preferred_element_type=jnp.float32
        ).astype(jnp.bfloat16)
        up(c).start()

    @pl.loop(0, CHUNKS)
    def _(c):
        load(0, c).wait()
        own = jnp.dot(latent_ref[...], dec[0, :, cols(c)], preferred_element_type=jnp.float32)
        up(c).wait_recv()
        carried = jnp.where(layer > 0, arrived[:, cols(c)].astype(jnp.float32), 0.0)
        sums[:, cols(c)] = (own + carried).astype(jnp.bfloat16)
        for q in range(1, m):
            for r in range(o):
                add_near(c, q, r).start()

    turned_ref[...] = acts_ref[...].T

    @pl.loop(0, CHUNKS)
    def _(c):
        for r in (*range(1, o), 0):
            total = sums[rows_of(at(r, 0)), cols(c)].astype(jnp.float32)
            for q in range(1, m):
                add_near(c, q, r).wait_recv()
                total = total + near[(q - 1) * o + r, :, cols(c)].astype(jnp.float32)
            if r:
                mids[r - 1, :, cols(c)] = total.astype(jnp.bfloat16)
                add_far(c, r).start()
            else:
                mine[:, cols(c)] = total

    @pl.loop(0, CHUNKS)
    def _(c):
        total = mine[:, cols(c)]
        for r in range(1, o):
            add_far(c, r).wait_recv()
            total = total + far[r - 1, :, cols(c)].astype(jnp.float32)
        errors = total + bias_ref[:, cols(c)] - targets_ref[:, cols(c)].astype(jnp.float32)
        errors_ref[:, cols(c)] = errors
        gath_ref[rows_of(me), cols(c)] = errors.astype(jnp.bfloat16)
        for r in range(1, o):
            give_far(c, r, me).start()
        for q in range(1, m):
            give_near(c, q, 0, me).start()
        down(c, 0, 0).start()

    @pl.loop(0, CHUNKS)
    def _(c):
        for r in range(1, o):
            owner = at(-r, 0)
            give_far(c, r, owner).wait_recv()
            for q in range(1, m):
                give_near(c, q, r, owner).start()
            down(c, 0, r).start()

    @pl.loop(0, CHUNKS)
    def _(c):
        for q in range(1, m):
            for r in range(o):
                give_near(c, q, r, at(-r, -q)).wait_recv()
                down(c, q, r).start()

    @pl.loop(0, CHUNKS)
    def _(c):
        up(c).wait_send()
        for r in range(1, o):
            add_far(c, r).wait_send()
            give_far(c, r, me).wait_send()
        for r in range(o):
            for q in range(1, m):
                add_near(c, q, r).wait_send()
                give_near(c, q, r, at(-r, 0)).wait_send()
            for q in range(m):
                down(c, q, r).wait_recv()
                down(c, q, r).wait_send()

    @pl.when(layer == layers - 1)
    def _():
        foll_ref[...] = jnp.zeros_like(foll_ref)


def exchange(layers, n, latent, dec, targets, bias, acts):
    tokens, features = latent.shape
    width = dec.shape[2]
    rows = tokens // n
    m = inner_of(n)
    o = n // m
    half = jnp.bfloat16
    vmem = pl.BlockSpec(memory_space=pltpu.VMEM)
    dma = pltpu.SemaphoreType.DMA
    pairs = [(CHUNKS, k) for k in ((m - 1) * o, o - 1, o - 1, (m - 1) * o, n)]
    return pl.pallas_call(
        functools.partial(exchange_kernel, layers, m, o),
        out_shape=(
            jax.ShapeDtypeStruct((rows, width), jnp.float32),
            jax.ShapeDtypeStruct((tokens, width), half),
            jax.ShapeDtypeStruct((tokens, width), half),
            jax.ShapeDtypeStruct((width, tokens), half),
        ),
        in_specs=[vmem, pl.BlockSpec(memory_space=pl.ANY), vmem, vmem, vmem],
        out_specs=(vmem, vmem, vmem, vmem),
        scratch_shapes=[
            pltpu.VMEM((2, features, width), half),
            pltpu.VMEM((tokens, width), half),
            pltpu.VMEM((tokens, width), half),
            pltpu.VMEM((tokens, width), half),
            pltpu.VMEM(((m - 1) * o, rows, width), half),
            pltpu.VMEM((o - 1, rows, width), half),
            pltpu.VMEM((o - 1, rows, width), half),
            pltpu.VMEM((rows, width), jnp.float32),
            dma((2, CHUNKS)),
            dma((CHUNKS,)),
            dma((CHUNKS,)),
            *[dma(p) for p in pairs for _ in range(2)],
        ],
        compiler_params=pltpu.CompilerParams(
            collective_id=0, has_side_effects=True, vmem_limit_bytes=48 * 2**20
        ),
        name="exchange",
    )(latent, dec, targets, bias, acts)


def grad_kernel(scale, gath_ref, foll_ref, turned_ref, dec_ref, pre_ref, out_ref):
    grad_latent = contract_width(gath_ref[...], dec_ref[0]) + contract_width(foll_ref[...], dec_ref[1])
    deriv = jax.nn.sigmoid(4.0 * pre_ref[...])
    grad_pre = (grad_latent * deriv).astype(jnp.bfloat16)
    total = jnp.dot(turned_ref[...], grad_pre, preferred_element_type=jnp.float32)
    out_ref[...] = (total * scale).astype(jnp.bfloat16)


def encoder_grad(gathered, following, turned, dec, pre):
    tokens, features = pre.shape
    width = turned.shape[0]
    tile = 256
    vmem = pl.BlockSpec(memory_space=pltpu.VMEM)
    return pl.pallas_call(
        functools.partial(grad_kernel, tokens ** (-0.5)),
        grid=(features // tile,),
        out_shape=jax.ShapeDtypeStruct((width, features), jnp.bfloat16),
        in_specs=[
            vmem, vmem, vmem,
            pl.BlockSpec((2, tile, width), lambda i: (0, i, 0)),
            pl.BlockSpec((tokens, tile), lambda i: (0, i)),
        ],
        out_specs=pl.BlockSpec((width, tile), lambda i: (0, i)),
        compiler_params=pltpu.CompilerParams(vmem_limit_bytes=40 * 2**20),
        name="encoder_grad",
    )(gathered, following, turned, dec, pre)


def contract_width(errs, decoder):
    return lax.dot_general(
        errs, decoder, (((1,), (1,)), ((), ())), preferred_element_type=jnp.float32
    )


def local(layers, n, acts, targets, enc_weight, enc_bias, dec_weight, dec_bias):
    inputs = acts[0]
    weight = enc_weight[0]
    bias = enc_bias[0]
    dec = jnp.transpose(dec_weight[0], (1, 0, 2))
    pre = jnp.dot(inputs, weight, preferred_element_type=jnp.float32) + bias
    latent = (jax.nn.softplus(4.0 * pre) * 0.25).astype(jnp.bfloat16)
    errors, gathered, following, turned = exchange(
        layers, n, latent, dec, targets[0], dec_bias, inputs
    )
    enc_grad = encoder_grad(gathered, following, turned, dec, pre)
    return (errors[None], enc_grad[None])


def solution(mesh):
    return jax.shard_map(
        functools.partial(local, mesh.shape["layer"], mesh.shape["feat"]),
        mesh=mesh,
        in_specs=(
            P("layer", None, None),
            P("layer", "feat", None),
            P("layer", None, "feat"),
            P("layer", "feat"),
            P("layer", "feat", None, None),
            P("layer", None),
        ),
        out_specs=(P("layer", "feat", None), P("layer", None, "feat")),
        check_vma=False,
    )
```

time: 145 us -> 127 us (0.88)
  matrix products: 35.5 us -> 15.9 us
  Pallas kernels: 87.6 us -> 97.3 us
  local copies, waits for them, and re-layouts: 20 us -> 12.1 us
    dot_general x2 -> x0, matrix products: 22.4 us -> none  [the longest x1 15.9 us: local(): lax.dot_general(inputs, grad_pre, (((0,), (0,)), ((), ())), preferred_ele...]
    pallas_call x1 -> x2, Pallas kernels: 87.6 us -> 97.3 us  [the longest x1 72.7 us: exchange(): pl.pallas_call(functools.partial(exchange_kernel, layers, m, o), out_shap...]
    unnamed x15 -> x8, local copies, waits for them, and re-layouts: 20 us -> 12.1 us
    dot_general x1, matrix products: 13.1 us -> 15.9 us  [local(): pre = jnp.dot(inputs, weight, preferred_element_type=jnp.float32) + bias]
where the time goes in v2:
time: 127 us
  Pallas kernels  97.3 us (77%)
  matrix products  15.9 us (13%)
  local copies, waits for them, and re-layouts  12.1 us (10%)
    pallas_call x1, Pallas kernels, exchange(): pl.pallas_call(functools.partial(exchange_kernel, layers, m, o), out_shap...  72.7 us
    pallas_call x1, Pallas kernels, encoder_grad(): pl.pallas_call(functools.partial(grad_kernel, tokens ** (-0.5)), grid=(fe...  24.6 us
    dot_general x1, matrix products, local(): pre = jnp.dot(inputs, weight, preferred_element_type=jnp.float32) + bias  15.9 us
    unnamed x8, local copies, waits for them, and re-layouts  12.1 us

profile of v2, /device:TPU:1, one launch (start us, length us, event | category | flops | bytes accessed | tf_op | source)
XLA Modules:
  0.0 126.6 jit_solution(4763825324734237872)
XLA Ops:
  0.6 0.7 reduce
  1.4 15.9 %fusion.1 = (bf16[768,2560]{1,0:T(8,128)(2,1)}, f32[768,2560]{1,0:T(8,128)}) fusion(f32[2560]{0:T(1024)S(1)} %reduce, bf16[1,1024,2560]{2,1,0:T(8,128)(2,1)} %param.8, bf16[1,768,1024]{2,1,0:T(8,128)(2,1)} %param.6), kind=kOutput, calls=%fused_computation.3 | convolution fusion | flops 4046192640 | bytes 18622464 | tf_op jit(solution)/shard_map/dot_general | solution.py:264
  17.2 0.0 copy-start.1
  17.2 0.0 copy-start.2
  17.3 11.3 %copy.10 = bf16[1,2560,2,1024]{3,1,2,0:T(8,128)(2,1)} copy(bf16[1,2560,2,1024]{3,2,1,0:T(2,128)(2,1)} %param.10) | data formatting | bytes 20971520 | tf_op args[4]
  28.6 0.0 copy-done.1
  28.6 0.0 copy-done.2
  28.6 0.0 copy-start
  28.6 72.7 %exchange.1 = (f32[96,1024]{1,0:T(8,128)S(1)}, bf16[768,1024]{1,0:T(8,128)(2,1)S(1)}, bf16[768,1024]{1,0:T(8,128)(2,1)S(1)}, bf16[1024,768]{1,0:T(8,128)(2,1)S(1)}) custom-call(bf16[768,2560]{1,0:T(8,128)(2,1)} %get-tuple-element.10.latent_ref, bf16[2,2560,1024]{2,1,0:T(8,128)(2,1)} %bitcast.20, bf16[96,1024]{1,0:T(8,128)(2,1)S(1)} %bitcast.19, ...), custom_call_target="tpu_custom_call" | custom-call | tf_op jit(solution)/shard_map/exchange/pallas_call | solution.py:194
  101.3 0.0 copy-done
  101.3 24.6 %encoder_grad.1 = bf16[1024,2560]{1,0:T(8,128)(2,1)} custom-call(bf16[768,1024]{1,0:T(8,128)(2,1)S(1)} %get-tuple-element.7.gath_ref, bf16[768,1024]{1,0:T(8,128)(2,1)S(1)} %get-tuple-element.8.foll_ref, bf16[1024,768]{1,0:T(8,128)(2,1)S(1)} %get-tuple-element.9.turned_ref, bf16[2,2560,1024]{2,1,0:T(8,128)(2,1)} %bitcast.21, f32[768,2560]{1,0:T(8,128)S(1)} %copy-done), custom_call_target="tpu_custom_call" | custom-call | tf_op jit(solution)/shard_map/encoder_grad/pallas_call | solution.py:238
  125.9 0.7 copy.12
Async XLA Ops:
  17.2 11.3 %copy-start.1 = (bf16[1,96,1024]{2,1,0:T(8,128)(2,1)S(1)}, bf16[1,96,1024]{2,1,0:T(8,128)(2,1)}, u32[]{:S(2)}) copy-start(bf16[1,96,1024]{2,1,0:T(8,128)(2,1)} %param.7) | copy-start | bytes 589828
  17.2 11.3 %copy-start.2 = (f32[1,1024]{1,0:T(1,128)S(1)}, f32[1,1024]{1,0:T(1,128)}, u32[]{:S(2)}) copy-start(f32[1,1024]{1,0:T(1,128)} %bias_ref.1) | copy-start | bytes 12292
  28.6 72.7 %copy-start = (f32[768,2560]{1,0:T(8,128)S(1)}, f32[768,2560]{1,0:T(8,128)}, u32[]{:S(2)}) copy-start(f32[768,2560]{1,0:T(8,128)} %get-tuple-element.11.pre_ref) | copy-start | bytes 23592964
